TPU v7x, 32 devices: a whole 2x2x4 slice. The times are simulated.
32 devices in a mesh: groups: 2 (over y), wide: 4 (over z), narrow: 2 (over x), section: 2 (over core).
Axes of the slice: x: 2, y: 2, z: 4, core: 2. Of those that a mesh axis runs over, the one named last changes fastest.
Arguments:
- tokens: bfloat16 [1024, 4096], P(('groups', 'wide', 'section'), 'narrow'), parts along dimension 0, may hold values from -6 to 6
- route_logits: float32 [1024, 8], P(('groups', 'wide', 'section')), parts along dimension 0, may hold values from -8 to 8
- expert_ids: int32 [1024, 8], P(('groups', 'wide', 'section')), parts along dimension 0, may hold values from 0 to 63, all different within a row; in each aligned block of 64 rows (0 to 63, 64 to 127, ...) at most 12 rows name the same one
- gate_weight: bfloat16 [64, 4096, 768], P(('wide', 'section'), None, 'narrow'), may hold values from -0.09375 to 0.09375
- up_weight: bfloat16 [64, 4096, 768], P(('wide', 'section'), None, 'narrow'), may hold values from -0.09375 to 0.09375
- down_weight: bfloat16 [64, 768, 4096], P(('wide', 'section'), None, 'narrow'), may hold values from -0.21875 to 0.21875
Outputs:
- mixed: bfloat16 [1024, 4096], P(('groups', 'wide', 'section'), 'narrow'), parts along dimension 0
There are 2 independent parts, one for each index of `groups`. A program takes and returns all parts, laid end to end along the dimension named above; an argument that names none is the same for every part. Nothing has to cross between parts.
Inputs may be any that keep to these rules, and one draw needn't show every extreme that they name: `expert_ids`: each row names 8 different experts; among the 64 rows of one aligned block no expert is named more than 12 times, a bound that some block reaches.
All inputs are finite; a program needn't handle non-finite values.
Results may differ from a plain program's by a relative error of at most 0.0085.
Values may be sent and summed in bfloat16 or wider, within the bound.
No kernel may reach another device: no remote copies, remote signals or barrier semaphores. Data moves between devices by JAX's collectives and lax.ppermute only.
A program may use at most 128 MiB of HBM per device.

v0:
```python
import jax
import jax.numpy as jnp
from jax import lax
from jax.sharding import PartitionSpec as P

CAP = 12


def shards(tokens, route_logits, expert_ids, gate_weight, up_weight, down_weight):
    tok_rows = tokens.shape[0]
    top_count = expert_ids.shape[1]
    feature_part = tokens.shape[1]
    wide_count = lax.axis_size("wide")
    section_count = lax.axis_size("section")
    owners = wide_count * section_count
    per_owner = gate_weight.shape[0]
    experts = owners * per_owner
    scores = jax.nn.sigmoid(route_logits)
    shares = (scores / jnp.sum(scores, axis=1, keepdims=True)).astype(jnp.bfloat16)
    flat_ids = expert_ids.reshape(-1)
    one_hot = (flat_ids[:, None] == jnp.arange(experts, dtype=jnp.int32)[None, :]).astype(jnp.int32)
    slot_rank = jnp.sum(jnp.cumsum(one_hot, axis=0) * one_hot, axis=1) - 1
    columns = flat_ids * CAP + slot_rank
    placed = (columns[:, None] == jnp.arange(experts * CAP, dtype=jnp.int32)[None, :]).reshape(
        tok_rows, top_count, experts * CAP
    )
    dispatch = jnp.any(placed, axis=1).astype(jnp.bfloat16)
    outgoing = jnp.einsum("rs,rd->sd", dispatch, tokens, preferred_element_type=jnp.float32).astype(
        jnp.bfloat16
    )
    combine = jnp.sum(
        jnp.where(placed, shares.astype(jnp.float32)[:, :, None], 0.0), axis=1
    ).astype(jnp.bfloat16)
    arrived = lax.all_to_all(
        outgoing.reshape(owners, per_owner, CAP, feature_part),
        ("wide", "section"),
        split_axis=0,
        concat_axis=0,
        tiled=True,
    )
    portion = lax.all_gather(arrived, "narrow", axis=3, tiled=True)
    gate_add = jnp.einsum(
        "gjcd,jdf->gjcf", portion, gate_weight, preferred_element_type=jnp.float32
    )
    up_add = jnp.einsum("gjcd,jdf->gjcf", portion, up_weight, preferred_element_type=jnp.float32)
    hidden = (jax.nn.silu(gate_add) * up_add).astype(jnp.bfloat16)
    summed = jnp.einsum(
        "gjcf,jfd->gjcd",
        lax.all_gather(hidden, "narrow", axis=3, tiled=True),
        down_weight,
        preferred_element_type=jnp.float32,
    ).astype(jnp.bfloat16)
    returned = lax.all_to_all(summed, ("wide", "section"), split_axis=0, concat_axis=0, tiled=True)
    returned = returned.reshape(experts * CAP, feature_part)
    return jnp.dot(combine, returned, preferred_element_type=jnp.float32).astype(jnp.bfloat16)


def solution(mesh):
    in_specs = (
        P(("groups", "wide", "section"), "narrow"),
        P(("groups", "wide", "section"), None),
        P(("groups", "wide", "section"), None),
        P(("wide", "section"), None, "narrow"),
        P(("wide", "section"), None, "narrow"),
        P(("wide", "section"), None, "narrow"),
    )
    out_specs = P(("groups", "wide", "section"), "narrow")
    return jax.shard_map(shards, mesh=mesh, in_specs=in_specs, out_specs=out_specs, check_vma=False)
```

profile of v0, /device:TPU:0, one launch (start us, length us, event | category | flops | bytes accessed | tf_op | source)
XLA Modules:
  0.0 370.5 jit_solution(8743993185270205982)
XLA Ops:
  6.5 0.0 copy-start
  6.5 0.0 all-gather.3.cloned.1.call-start
  6.5 0.8 copy.38
  7.4 0.1 eq.43
  7.4 0.1 eq.39
  7.6 1.2 reduce-window.6
  8.8 0.2 slice_reduce_fusion
  9.0 0.1 fusion.18
  9.2 0.1 sub.7
  9.3 0.1 copy.41
  9.3 0.7 multiply_add_fusion
  10.0 0.1 copy.42
  10.1 0.5 fusion.14
  10.7 0.0 copy-done
  10.7 1.0 convolution_convert_fusion
  11.7 2.7 reshape.47
  14.4 4.0 %copy.44 = bf16[8,8,12,2048]{3,1,2,0:T(8,128)(2,1)S(1)} copy(bf16[8,8,12,2048]{3,2,1,0:T(8,128)(2,1)} %reshape.47) | data formatting | bytes 6291456 | tf_op jit(solution)/shard_map/reshape | solution.py:35
  18.4 77.7 %all_to_all.10 = bf16[8,8,12,2048]{3,1,2,0:T(8,128)(2,1)S(1)} all-to-all(bf16[8,8,12,2048]{3,1,2,0:T(8,128)(2,1)S(1)} %copy.44), channel_id=1, replica_groups=mesh['groups'=2,'wide'=4,'narrow'=2,'section'=2] {'wide','section'}, dimensions={0} | all-to-all | bytes 6291456 | tf_op jit(solution)/shard_map/all_to_all | solution.py:34
  96.0 3.8 %copy.45 = bf16[8,8,12,2048]{3,2,0,1:T(8,128)(2,1)} copy(bf16[8,8,12,2048]{3,1,2,0:T(8,128)(2,1)S(1)} %all_to_all.10) | data formatting | bytes 6291456 | tf_op jit(solution)/shard_map/all_to_all | solution.py:34
  99.8 0.0 all-gather.3.cloned.1.call-update
  99.8 0.2 all-gather.5.cloned.1.call-start
  100.1 102.8 %all-gather.3.cloned.1.call-done = bf16[8,8,12,4096]{3,2,0,1:T(8,128)(2,1)} async-done(((bf16[8,8,12,2048]{3,2,0,1:T(8,128)(2,1)}), bf16[8,8,12,4096]{3,2,0,1:T(8,128)(2,1)}) %all-gather.3.cloned.1.call-update) | async-done | bytes 6291472 | tf_op jit(solution)/shard_map/all_gather | solution.py:41
  202.9 15.2 %bitcast_multiply_fusion.1 = f32[8,8,12,384]{3,2,0,1:T(8,128)S(1)} fusion(bf16[8,8,12,4096]{3,2,0,1:T(8,128)(2,1)} %all-gather.3.cloned.1.call-done, bf16[8,4096,384]{2,1,0:T(8,128)(2,1)} %param.9), kind=kOutput, calls=%fused_computation.11 | convolution fusion | flops 2417098752 | bytes 32636928 | tf_op jit(solution)/shard_map/gjcd,jdf->gjcf/dot_general | solution.py:42
  218.1 16.1 %fusion.8 = bf16[8,8,12,384]{3,2,0,1:T(8,128)(2,1)} fusion(f32[8,8,12,384]{3,2,0,1:T(8,128)S(1)} %bitcast_multiply_fusion.1, bf16[8,8,12,4096]{3,2,0,1:T(8,128)(2,1)} %all-gather.3.cloned.1.call-done, bf16[8,4096,384]{2,1,0:T(8,128)(2,1)} %param.10), kind=kOutput, calls=%fused_computation.10 | convolution fusion | flops 2416508928 | bytes 33226752 | tf_op jit(solution)/shard_map/gjcd,jdf->gjcf/dot_general | solution.py:45
  234.2 0.0 all-gather.5.cloned.1.call-update
  234.2 27.3 %all-gather.5.cloned.1.call-done = bf16[8,8,12,768]{3,2,0,1:T(8,128)(2,1)} async-done(((bf16[8,8,12,384]{3,2,0,1:T(8,128)(2,1)}), bf16[8,8,12,768]{3,2,0,1:T(8,128)(2,1)}) %all-gather.5.cloned.1.call-update) | async-done | bytes 1179664 | tf_op jit(solution)/shard_map/all_gather | solution.py:49
  261.6 12.3 %convert_bitcast_fusion = bf16[8,8,12,2048]{3,2,0,1:T(8,128)(2,1)S(1)} fusion(bf16[8,8,12,768]{3,2,0,1:T(8,128)(2,1)} %all-gather.5.cloned.1.call-done, bf16[8,768,2048]{2,1,0:T(8,128)(2,1)} %param.11), kind=kOutput, calls=%fused_computation.6 | convolution fusion | flops 2417491968 | bytes 29491200 | tf_op jit(solution)/shard_map/gjcf,jfd->gjcd/dot_general | solution.py:47
  273.9 3.5 copy.46
  277.4 0.0 copy-start.2
  277.4 4.7 %all-to-all-start.1 = ((bf16[8,8,12,2048]{3,1,2,0:T(8,128)(2,1)}), bf16[8,8,12,2048]{3,1,2,0:T(8,128)(2,1)S(1)}, u32[]{:S(2)}, u32[]{:S(2)}) async-start(bf16[8,8,12,2048]{3,1,2,0:T(8,128)(2,1)} %copy.46), calls=%async_computation.1 | async-start | bytes 6291456 | tf_op jit(solution)/shard_map/all_to_all | solution.py:53
  282.1 0.0 copy-done.2
  282.2 0.1 copy.43
  282.2 0.6 select_reduce_fusion
  282.8 70.8 %all-to-all-done.1 = bf16[8,8,12,2048]{3,1,2,0:T(8,128)(2,1)S(1)} async-done(((bf16[8,8,12,2048]{3,1,2,0:T(8,128)(2,1)}), bf16[8,8,12,2048]{3,1,2,0:T(8,128)(2,1)S(1)}, u32[]{:S(2)}, u32[]{:S(2)}) %all-to-all-start.1) | async-done | bytes 3145760 | tf_op jit(solution)/shard_map/all_to_all | solution.py:53
  353.6 3.9 %copy.47 = bf16[8,8,12,2048]{3,2,1,0:T(8,128)(2,1)} copy(bf16[8,8,12,2048]{3,1,2,0:T(8,128)(2,1)S(1)} %all-to-all-done.1) | data formatting | bytes 6291456 | tf_op jit(solution)/shard_map/all_to_all | solution.py:53
  357.5 0.0 copy-start.1
  357.5 4.8 %reshape.48 = bf16[768,2048]{1,0:T(8,128)(2,1)S(1)} reshape(bf16[8,8,12,2048]{3,2,1,0:T(8,128)(2,1)} %copy.47) | data formatting | bytes 6291456 | tf_op jit(solution)/shard_map/reshape | solution.py:54
  362.2 1.4 convolution_convert_fusion.1
  363.6 0.0 copy-done.1
  (6 shorter events, 0.1 us)
Async XLA Ops:
  6.5 4.1 %copy-start = (bf16[64,2048]{1,0:T(8,128)(2,1)S(1)}, bf16[64,2048]{1,0:T(8,128)(2,1)}, u32[]{:S(2)}) copy-start(bf16[64,2048]{1,0:T(8,128)(2,1)} %param.6) | copy-start | bytes 786436
  6.5 196.4 %all-gather.3.cloned.1.call-start = ((), (), s32[]{:S(2)}) async-start(), calls=%async_computation.2 | async-start | bytes 12582912 | tf_op jit(solution)/shard_map/all_gather | solution.py:41
  99.8 161.7 %all-gather.5.cloned.1.call-start = ((), (), s32[]{:S(2)}) async-start(), calls=%async_computation.3 | async-start | bytes 2359296 | tf_op jit(solution)/shard_map/all_gather | solution.py:49
  277.4 4.7 %copy-start.2 = (f32[64,8]{0,1:T(8,128)S(1)}, f32[64,8]{0,1:T(8,128)}, u32[]{:S(2)}) copy-start(f32[64,8]{0,1:T(8,128)} %param.7) | copy-start | bytes 6148
  277.4 76.2 %all-to-all-start.1 = ((bf16[8,8,12,2048]{3,1,2,0:T(8,128)(2,1)}), bf16[8,8,12,2048]{3,1,2,0:T(8,128)(2,1)S(1)}, u32[]{:S(2)}, u32[]{:S(2)}) async-start(bf16[8,8,12,2048]{3,1,2,0:T(8,128)(2,1)} %copy.46), calls=%async_computation.1 | async-start | bytes 6291456 | tf_op jit(solution)/shard_map/all_to_all | solution.py:53
  357.5 6.1 %copy-start.1 = (bf16[64,2048]{1,0:T(8,128)(2,1)S(1)}, bf16[64,2048]{1,0:T(8,128)(2,1)}, u32[]{:S(2)}) copy-start(bf16[64,2048]{1,0:T(8,128)(2,1)} %param.6) | copy-start | bytes 786436
Sparse Core Ops, SparseCore 0:
  99.9 102.9 all-gather.2
  234.3 27.1 all-gather.4
where the time goes:
time: 371 us; the launch traced here: 370 us
  waiting for transfers between devices  201 us (54%)
  blocking collectives  77.7 us (21%)
  matrix products  46 us (12%)
  local copies, waits for them, and re-layouts  24.1 us (6%)
  between operations  13.5 us (4%)
  starting transfers between devices  4.97 us (1%)
    all_gather x1, waiting for transfers between devices, shards(): portion = lax.all_gather(arrived, 'narrow', axis=3, tiled=True)  103 us
    all_to_all x1, blocking collectives, shards(): lax.all_to_all(outgoing.reshape(owners, per_owner, CAP, feature_part), ('...  77.7 us
    all_to_all x1, waiting for transfers between devices, shards(): lax.all_to_all(summed, ('wide', 'section'), split_axis=0, concat_axis=0,...  70.8 us
    all_gather x1, waiting for transfers between devices, shards(): lax.all_gather(hidden, 'narrow', axis=3, tiled=True)  27.3 us
    dot_general x1, matrix products, shards(): jnp.einsum('gjcd,jdf->gjcf', portion, up_weight, preferred_element_type=j...  16.1 us
    dot_general x1, matrix products, shards(): jnp.einsum('gjcd,jdf->gjcf', portion, gate_weight, preferred_element_type...  15.2 us
    dot_general x1, matrix products, shards(): jnp.einsum('gjcf,jfd->gjcd', lax.all_gather(hidden, 'narrow', axis=3, til...  12.3 us
  transfers between devices with their start and end apart: 3, of which 3 were waited for; matrix products, arithmetic and copies ran while one was open for 0% of the time, Pallas kernels for 0%

commit v1 on v0

--- a/solution.py
+++ b/solution.py
@@ -4,6 +4,18 @@
 from jax.sharding import PartitionSpec as P
 
 CAP = 12
+
+
+def collect(x, axis, dim):
+    ways, here, step = (lax.axis_size(axis), lax.axis_index(axis), x.shape[dim])
+    line, have = (x, 1)
+    while have < ways:
+        line = jnp.concatenate(
+            [line, lax.ppermute(line, axis, [(d, (d - have) % ways) for d in range(ways)])],
+            axis=dim,
+        )
+        have = 2 * have
+    return jnp.roll(line, here * step, axis=dim)
 
 
 def shards(tokens, route_logits, expert_ids, gate_weight, up_weight, down_weight):
@@ -46,7 +58,7 @@
     hidden = (jax.nn.silu(gate_add) * up_add).astype(jnp.bfloat16)
     summed = jnp.einsum(
         "gjcf,jfd->gjcd",
-        lax.all_gather(hidden, "narrow", axis=3, tiled=True),
+        collect(hidden, "narrow", 3),
         down_weight,
         preferred_element_type=jnp.float32,
     ).astype(jnp.bfloat16)

time: 371 us -> 364 us (0.981)
  waiting for transfers between devices: 201 us -> 188 us
    all_gather x1 -> x0, waiting for transfers between devices: 27.3 us -> none  [shards(): lax.all_gather(hidden, 'narrow', axis=3, tiled=True)]
    ppermute x0 -> x1, waiting for transfers between devices: none -> 14.6 us  [collect(): lax.ppermute(line, axis, [(d, (d - have) % ways) for d in range(ways)])]
where the time goes in v1:
time: 364 us; the launch traced here: 363 us
  waiting for transfers between devices  188 us (52%)
  blocking collectives  77.7 us (21%)
  matrix products  48.3 us (13%)
  local copies, waits for them, and re-layouts  26.9 us (7%)
  between operations  13.5 us (4%)
  starting transfers between devices  5.15 us (1%)
    all_gather x1, waiting for transfers between devices, shards(): portion = lax.all_gather(arrived, 'narrow', axis=3, tiled=True)  103 us
    all_to_all x1, blocking collectives, shards(): lax.all_to_all(outgoing.reshape(owners, per_owner, CAP, feature_part), ('...  77.7 us
    all_to_all x1, waiting for transfers between devices, shards(): lax.all_to_all(summed, ('wide', 'section'), split_axis=0, concat_axis=0,...  70.8 us
    dot_general x1, matrix products, shards(): jnp.einsum('gjcf,jfd->gjcd', collect(hidden, 'narrow', 3), down_weight, p...  15.6 us
    dot_general x1, matrix products, shards(): jnp.einsum('gjcd,jdf->gjcf', portion, gate_weight, preferred_element_type...  15.2 us
    dot_general x1, matrix products, shards(): jnp.einsum('gjcd,jdf->gjcf', portion, up_weight, preferred_element_type=j...  15.1 us
    ppermute x1, waiting for transfers between devices, collect(): lax.ppermute(line, axis, [(d, (d - have) % ways) for d in range(ways)])  14.6 us
  transfers between devices with their start and end apart: 3, of which 3 were waited for; matrix products, arithmetic and copies ran while one was open for 0% of the time, Pallas kernels for 0%

profile of v1, /device:TPU:0, one launch (start us, length us, event | category | flops | bytes accessed | tf_op | source)
XLA Modules:
  0.0 363.2 jit_solution(5777854912567323225)
XLA Ops:
  6.5 0.0 copy-start
  6.5 0.0 all-gather.2.cloned.1.call-start
  6.5 0.8 copy.44
  7.4 0.1 eq.46
  7.4 0.1 eq.42
  7.6 1.2 reduce-window.6
  8.8 0.2 slice_reduce_fusion
  9.0 0.1 fusion.22
  9.2 0.1 sub.11
  9.3 0.1 copy.47
  9.3 0.7 multiply_add_fusion
  10.0 0.1 copy.48
  10.1 0.5 fusion.18
  10.7 0.0 copy-done
  10.7 1.0 convolution_convert_fusion
  11.7 2.7 reshape.47
  14.4 4.0 %copy.50 = bf16[8,8,12,2048]{3,1,2,0:T(8,128)(2,1)S(1)} copy(bf16[8,8,12,2048]{3,2,1,0:T(8,128)(2,1)} %reshape.47) | data formatting | bytes 6291456 | tf_op jit(solution)/shard_map/reshape | solution.py:47
  18.4 77.7 %all_to_all.10 = bf16[8,8,12,2048]{3,1,2,0:T(8,128)(2,1)S(1)} all-to-all(bf16[8,8,12,2048]{3,1,2,0:T(8,128)(2,1)S(1)} %copy.50), channel_id=1, replica_groups=mesh['groups'=2,'wide'=4,'narrow'=2,'section'=2] {'wide','section'}, dimensions={0} | all-to-all | bytes 6291456 | tf_op jit(solution)/shard_map/all_to_all | solution.py:46
  96.0 3.8 %copy.51 = bf16[8,8,12,2048]{3,2,0,1:T(8,128)(2,1)} copy(bf16[8,8,12,2048]{3,1,2,0:T(8,128)(2,1)S(1)} %all_to_all.10) | data formatting | bytes 6291456 | tf_op jit(solution)/shard_map/all_to_all | solution.py:46
  99.8 0.0 all-gather.2.cloned.1.call-update
  99.8 103.1 %all-gather.2.cloned.1.call-done = bf16[8,8,12,4096]{3,2,0,1:T(8,128)(2,1)} async-done(((bf16[8,8,12,2048]{3,2,0,1:T(8,128)(2,1)}), bf16[8,8,12,4096]{3,2,0,1:T(8,128)(2,1)}) %all-gather.2.cloned.1.call-update) | async-done | bytes 6291472 | tf_op jit(solution)/shard_map/all_gather | solution.py:53
  202.9 15.2 %bitcast_multiply_fusion.1 = f32[8,8,12,384]{3,2,0,1:T(8,128)S(1)} fusion(bf16[8,8,12,4096]{3,2,0,1:T(8,128)(2,1)} %all-gather.2.cloned.1.call-done, bf16[8,4096,384]{2,1,0:T(8,128)(2,1)} %param.9), kind=kOutput, calls=%fused_computation.18 | convolution fusion | flops 2417098752 | bytes 32636928 | tf_op jit(solution)/shard_map/gjcd,jdf->gjcf/dot_general | solution.py:54
  218.1 15.1 %fusion.12 = bf16[8,8,12,384]{3,2,0,1:T(8,128)(2,1)S(1)} fusion(f32[8,8,12,384]{3,2,0,1:T(8,128)S(1)} %bitcast_multiply_fusion.1, bf16[8,8,12,4096]{3,2,0,1:T(8,128)(2,1)} %all-gather.2.cloned.1.call-done, bf16[8,4096,384]{2,1,0:T(8,128)(2,1)} %param.10), kind=kOutput, calls=%fused_computation.17 | convolution fusion | flops 2416508928 | bytes 33226752 | tf_op jit(solution)/shard_map/gjcd,jdf->gjcf/dot_general | solution.py:57
  233.3 0.3 copy.52
  233.6 0.4 collective-permute-start
  234.0 14.6 %collective-permute-done = bf16[8,8,12,384]{3,1,2,0:T(8,128)(2,1)S(1)} collective-permute-done((bf16[8,8,12,384]{3,1,2,0:T(8,128)(2,1)S(1)}, bf16[8,8,12,384]{3,1,2,0:T(8,128)(2,1)S(1)}, u32[]{:S(2)}, u32[]{:S(2)}) %collective-permute-start) | collective-permute-done | bytes 589856 | tf_op jit(solution)/shard_map/ppermute | solution.py:14
  248.6 0.1 copy.53
  248.7 15.6 %convert_bitcast_fusion = bf16[8,8,12,2048]{3,2,0,1:T(8,128)(2,1)} fusion(bf16[8,768,2048]{2,1,0:T(8,128)(2,1)} %param.11, s32[]{:T(128)S(6)} %select_n.19, bf16[8,8,12,384]{3,2,0,1:T(8,128)(2,1)S(1)} %fusion.12, bf16[8,8,12,384]{3,2,0,1:T(8,128)(2,1)S(1)} %copy.53), kind=kOutput, calls=%fused_computation.6 | convolution fusion | flops 2422210560 | bytes 29491204 | tf_op jit(solution)/shard_map/gjcf,jfd->gjcd/dot_general | solution.py:59
  264.3 5.9 %copy.55 = bf16[8,8,12,2048]{3,1,2,0:T(8,128)(2,1)} copy(bf16[8,8,12,2048]{3,2,0,1:T(8,128)(2,1)} %convert_bitcast_fusion) | data formatting | bytes 6291456 | tf_op jit(solution)/shard_map/convert_element_type | solution.py:64
  270.1 0.0 copy-start.2
  270.1 4.7 %all-to-all-start.1 = ((bf16[8,8,12,2048]{3,1,2,0:T(8,128)(2,1)}), bf16[8,8,12,2048]{3,1,2,0:T(8,128)(2,1)S(1)}, u32[]{:S(2)}, u32[]{:S(2)}) async-start(bf16[8,8,12,2048]{3,1,2,0:T(8,128)(2,1)} %copy.55), calls=%async_computation.1 | async-start | bytes 6291456 | tf_op jit(solution)/shard_map/all_to_all | solution.py:65
  274.9 0.0 copy-done.2
  274.9 0.1 copy.49
  275.0 0.6 select_reduce_fusion
  275.6 70.8 %all-to-all-done.1 = bf16[8,8,12,2048]{3,1,2,0:T(8,128)(2,1)S(1)} async-done(((bf16[8,8,12,2048]{3,1,2,0:T(8,128)(2,1)}), bf16[8,8,12,2048]{3,1,2,0:T(8,128)(2,1)S(1)}, u32[]{:S(2)}, u32[]{:S(2)}) %all-to-all-start.1) | async-done | bytes 3145760 | tf_op jit(solution)/shard_map/all_to_all | solution.py:65
  346.4 3.9 %copy.56 = bf16[8,8,12,2048]{3,2,1,0:T(8,128)(2,1)} copy(bf16[8,8,12,2048]{3,1,2,0:T(8,128)(2,1)S(1)} %all-to-all-done.1) | data formatting | bytes 6291456 | tf_op jit(solution)/shard_map/all_to_all | solution.py:65
  350.2 0.0 copy-start.1
  350.2 4.8 %reshape.48 = bf16[768,2048]{1,0:T(8,128)(2,1)S(1)} reshape(bf16[8,8,12,2048]{3,2,1,0:T(8,128)(2,1)} %copy.56) | data formatting | bytes 6291456 | tf_op jit(solution)/shard_map/reshape | solution.py:66
  355.0 1.4 convolution_convert_fusion.1
  356.4 0.0 copy-done.1
  (6 shorter events, 0.1 us)
Async XLA Ops:
  6.5 4.1 %copy-start = (bf16[64,2048]{1,0:T(8,128)(2,1)S(1)}, bf16[64,2048]{1,0:T(8,128)(2,1)}, u32[]{:S(2)}) copy-start(bf16[64,2048]{1,0:T(8,128)(2,1)} %param.6) | copy-start | bytes 786436
  6.5 196.4 %all-gather.2.cloned.1.call-start = ((), (), s32[]{:S(2)}) async-start(), calls=%async_computation.2 | async-start | bytes 12582912 | tf_op jit(solution)/shard_map/all_gather | solution.py:53
  233.6 15.0 %collective-permute-start = (bf16[8,8,12,384]{3,1,2,0:T(8,128)(2,1)S(1)}, bf16[8,8,12,384]{3,1,2,0:T(8,128)(2,1)S(1)}, u32[]{:S(2)}, u32[]{:S(2)}) collective-permute-start(bf16[8,8,12,384]{3,1,2,0:T(8,128)(2,1)S(1)} %copy.52), channel_id=1, source_target_pairs={{0,2},{2,0},{1,3},{3,1},{4,6},{6,4},{5,7},{7,5},{8,10},{10,8},{9,1... | collective-permute-start | bytes 1769480 | tf_op jit(solution)/shard_map/ppermute | solution.py:14
  270.1 4.7 %copy-start.2 = (f32[64,8]{0,1:T(8,128)S(1)}, f32[64,8]{0,1:T(8,128)}, u32[]{:S(2)}) copy-start(f32[64,8]{0,1:T(8,128)} %param.7) | copy-start | bytes 6148
  270.1 76.2 %all-to-all-start.1 = ((bf16[8,8,12,2048]{3,1,2,0:T(8,128)(2,1)}), bf16[8,8,12,2048]{3,1,2,0:T(8,128)(2,1)S(1)}, u32[]{:S(2)}, u32[]{:S(2)}) async-start(bf16[8,8,12,2048]{3,1,2,0:T(8,128)(2,1)} %copy.55), calls=%async_computation.1 | async-start | bytes 6291456 | tf_op jit(solution)/shard_map/all_to_all | solution.py:65
  350.2 6.1 %copy-start.1 = (bf16[64,2048]{1,0:T(8,128)(2,1)S(1)}, bf16[64,2048]{1,0:T(8,128)(2,1)}, u32[]{:S(2)}) copy-start(bf16[64,2048]{1,0:T(8,128)(2,1)} %param.6) | copy-start | bytes 786436
Sparse Core Ops, SparseCore 0:
  99.9 102.9 all-gather.1
